TPU v7x, 32 devices: a whole 2x2x4 slice. The times are simulated.
32 devices in a mesh: orb: 8 (over z, y), slab: 4 (over x, core).
Axes of the slice: x: 2, y: 2, z: 4, core: 2. Of those that a mesh axis runs over, the one named last changes fastest.
Arguments:
- orbitals: float32 [2, 1024, 16384], P(None, 'orb', 'slab'), may hold values from -1.5 to 1.5
- offsets: int32 [1024], replicated, may hold values from 0 to 1472, as said below
- pairs: int32 [8, 3], P('orb'), may hold values from 0 to 1, as said below
- kernel: float32 [8, 3, 128, 128], P('orb'), may hold values from -0.6 to 0.6
Outputs:
- gradient: float32 [1024, 16384], P('orb', 'slab')
Inputs may be any that keep to these rules, and one draw needn't show every extreme that they name: offsets[f] lies between 192 * (f // 128) and 192 * (f // 128) + 128; in every block the first function's offset is the low end and the second function's the high end. pairs[A, 1] is 1; the list is symmetric, pairs[A, 1 + k] = pairs[A + k, 1 - k]; entries whose block A + k lies outside 0 to 7 are 0.
All inputs are finite; a program needn't handle non-finite values.
Results may differ from a plain program's by a relative error of at most 0.0003.
Values sent between devices are 32-bit elements; how exact they have to be, the bound alone decides.
No kernel may reach another device: no remote copies, remote signals or barrier semaphores. Data moves between devices by JAX's collectives and lax.ppermute only.
A program may use at most 128 MiB of HBM per device.

v0:
```python
import math

import jax
import jax.numpy as jnp
from jax import lax
from jax.sharding import PartitionSpec as P

BLOCK_FUNCTIONS = 128
PATCH = 256
SPREAD = 128
REACH = 1
BSTEP = 192
SEG = 16384


def passed_along(value, axis, steps):
    count = lax.axis_size(axis)
    first, last = (max(0, -steps), min(count, count - steps))
    return lax.ppermute(value, axis, [(source, source + steps) for source in range(first, last)])


def position_row(segment, column_shift, window):
    blank = jnp.zeros((segment.shape[0], window), segment.dtype)
    return lax.dynamic_update_slice(blank, segment, (jnp.int32(0), column_shift))


def place_rows(segments, shifts, window):

    def inner(member_rows):
        return jax.vmap(lambda segment, column_shift: position_row(segment, column_shift, window))(
            member_rows, shifts
        )

    return jax.vmap(inner)(segments)


def pick_row(window_row, column_shift, patch):
    return lax.dynamic_slice(window_row, (jnp.int32(0), column_shift), (window_row.shape[0], patch))


def aligned(own_part, near_part, lag_cols):
    window = own_part.shape[-1]
    if lag_cols >= 0:
        return (own_part[..., lag_cols:], near_part[..., : window - lag_cols])
    return (own_part[..., : window + lag_cols], near_part[..., -lag_cols:])


def per_device(orbitals, offsets, pairs, kernel):
    members, per_dev, seg_local = orbitals.shape
    planes = seg_local // PATCH
    window = PATCH + SPREAD
    blocks_dev = per_dev // BLOCK_FUNCTIONS
    reach_blocks = REACH
    edge_rows = reach_blocks * BLOCK_FUNCTIONS
    first_row = lax.axis_index("orb") * per_dev
    segments = orbitals.reshape(members, per_dev, planes, PATCH)
    own_rows = first_row + jnp.arange(per_dev, dtype=jnp.int32)
    own_offsets = lax.dynamic_slice_in_dim(offsets, first_row, per_dev)
    own_shift = jnp.clip(own_offsets - BSTEP * (own_rows // BLOCK_FUNCTIONS), 0, SPREAD)
    own_windows = place_rows(segments, own_shift, window)
    own_split = own_windows.reshape(members, blocks_dev, BLOCK_FUNCTIONS, planes, window)
    widths = window - BSTEP
    to_lower = own_split[:, 0, ..., :widths]
    to_upper = own_split[:, blocks_dev - 1, ..., window - widths :]
    upper_source = passed_along(to_lower, "orb", -1)
    from_lower = passed_along(to_upper, "orb", 1)
    lower_blocks = []
    pad_cols = window - widths
    upper_blocks = [jnp.pad(upper_source, ((0, 0), (0, 0), (0, 0), (0, pad_cols)))]
    lower_blocks.insert(0, jnp.pad(from_lower, ((0, 0), (0, 0), (0, 0), (pad_cols, 0))))
    lower_part = jnp.stack(lower_blocks, axis=1).reshape(members, edge_rows, planes, window)
    upper_part = jnp.stack(upper_blocks, axis=1).reshape(members, edge_rows, planes, window)
    neighbours = jnp.concatenate([lower_part, own_windows, upper_part], axis=1)
    own_blocks = own_windows.reshape(members, blocks_dev, BLOCK_FUNCTIONS, planes, window)
    near_blocks = neighbours.reshape(
        members, blocks_dev + 2 * reach_blocks, BLOCK_FUNCTIONS, planes, window
    )
    volume = 1.0 / math.sqrt(SEG)
    slab_terms = []
    for block_distance in range(-reach_blocks, reach_blocks + 1):
        first_block = reach_blocks + block_distance
        nearby = near_blocks[:, first_block : first_block + blocks_dev]
        own_part, near_part = aligned(own_blocks[0], nearby[1], block_distance * BSTEP)
        slab_terms.append(
            volume
            * jnp.einsum("bixc,bjxc->bij", own_part, near_part, precision=lax.Precision.HIGHEST)
        )
    margin_sums = lax.psum(jnp.stack(slab_terms, axis=1), "slab")
    weight = pairs.astype(jnp.float32)[:, :, None, None]
    kernel_rows = kernel * weight
    hamilton_rows = margin_sums * weight
    accumulated = jnp.zeros((blocks_dev, BLOCK_FUNCTIONS, planes, window), jnp.float32)
    for block_distance in range(-reach_blocks, reach_blocks + 1):
        slot_index = block_distance + reach_blocks
        first_block = reach_blocks + block_distance
        nearby = near_blocks[:, first_block : first_block + blocks_dev]
        lag_cols = block_distance * BSTEP
        if lag_cols >= 0:
            target = slice(lag_cols, window)
            source = slice(0, window - lag_cols)
        else:
            target = slice(0, window + lag_cols)
            source = slice(-lag_cols, window)
        both_rows = jnp.stack([-hamilton_rows[:, slot_index], kernel_rows[:, slot_index]], axis=1)
        contribution = jnp.einsum(
            "bmij,mbjxc->bixc", both_rows, nearby[..., source], precision=lax.Precision.HIGHEST
        )
        accumulated = accumulated.at[..., target].add(contribution)
    picked = jax.vmap(lambda window_row, column_shift: pick_row(window_row, column_shift, PATCH))(
        accumulated.reshape(per_dev, planes, window), own_shift
    )
    return picked.reshape(per_dev, planes * PATCH)


def solution(mesh):
    placed = (P(None, "orb", "slab"), P(), P("orb", None), P("orb", None, None, None))
    return jax.shard_map(
        per_device, mesh=mesh, in_specs=placed, out_specs=P("orb", "slab"), check_vma=False
    )
```

profile of v0, /device:TPU:0, one launch (start us, length us, event | category | flops | bytes accessed | tf_op | source)
XLA Modules:
  0.0 1475.1 jit_solution(12529493140982271850)
XLA Ops:
  6.5 3.9 copy.57
  14.0 3.1 broadcast_in_dim.12
  17.1 1141.0 %while.5 = (s32[]{:T(128)}, f32[2,128,16,384]{3,2,1,0:T(8,128)}, s32[128,3]{0,1:T(4,128)S(1)}, f32[128,2,16,256]{3,2,1,0:T(8,128)}, s32[]{:T(128)}, /*index=5*/s32[4]{0:T(128)S(1)}, s32[1]{0:T(128)}, s32[]{:T(128)}) while((s32[]{:T(128)}, f32[2,128,16,384]{3,2,1,0:T(8,128)}, s32[128,3]{0,1:T(4,128)S(1)}, f32[128,2,16,256]{3,2,1,0:T(8,128)}, ...), condition=%wide.while_cond.3, body=%wide.while_body.3.sunk | while | flops 8221 | bytes 164027 | solution.py:24
  40.3 3.0 dynamic-update-slice.12
  49.2 3.0 dynamic-update-slice.12
  58.1 3.0 dynamic-update-slice.12
  67.1 3.0 dynamic-update-slice.12
  111.7 3.0 dynamic-update-slice.12
  120.6 3.0 dynamic-update-slice.12
  156.3 3.0 dynamic-update-slice.12
  174.2 3.0 dynamic-update-slice.12
  200.9 3.0 dynamic-update-slice.12
  245.6 3.0 dynamic-update-slice.12
  254.5 3.0 dynamic-update-slice.12
  325.5 3.0 dynamic-update-slice.12
  343.4 3.0 dynamic-update-slice.12
  379.1 3.0 dynamic-update-slice.12
  388.0 3.0 dynamic-update-slice.12
  414.8 3.0 dynamic-update-slice.12
  468.3 3.0 dynamic-update-slice.12
  646.5 3.0 dynamic-update-slice.12
  655.4 3.0 dynamic-update-slice.12
  673.3 3.0 dynamic-update-slice.12
  744.6 3.0 dynamic-update-slice.12
  780.3 3.0 dynamic-update-slice.12
  789.2 3.0 dynamic-update-slice.12
  878.5 3.0 dynamic-update-slice.12
  932.0 3.0 dynamic-update-slice.12
  940.9 3.0 dynamic-update-slice.12
  949.9 3.0 dynamic-update-slice.12
  976.6 3.0 dynamic-update-slice.12
  985.6 3.0 dynamic-update-slice.12
  1021.3 3.0 dynamic-update-slice.12
  1030.2 3.0 dynamic-update-slice.12
  1039.1 3.0 dynamic-update-slice.12
  1048.1 3.0 dynamic-update-slice.12
  1083.8 3.0 dynamic-update-slice.12
  1092.7 3.0 dynamic-update-slice.12
  1110.6 3.0 dynamic-update-slice.12
  1158.1 6.6 copy.30
  1164.7 5.3 slice_bitcast_fusion.3
  1170.0 6.5 collective-permute-start
  1178.5 4.6 copy.35
  1183.0 126.6 %collective-permute-done = f32[2,128,16,192]{1,3,2,0:T(8,128)} collective-permute-done((f32[2,128,16,192]{1,3,2,0:T(8,128)S(1)}, f32[2,128,16,192]{1,3,2,0:T(8,128)}, u32[]{:S(2)}, u32[]{:S(2)}) %collective-permute-start) | collective-permute-done | bytes 3145760 | tf_op jit(solution)/shard_map/ppermute | solution.py:19
  1309.6 5.1 copy.32
  1314.8 3.4 copy.33
  1318.2 6.5 select_maximum_fusion
  1324.7 4.0 fusion.37
  1328.7 5.3 copy-done
  1334.0 3.6 copy.51
  1337.6 4.7 fusion.23
  1344.9 4.7 fusion.21
  1349.5 5.2 fusion.19
  1355.5 8.0 fusion.36
  1363.5 5.8 slice.211
  1369.3 5.0 copy.54
  1374.3 3.7 copy.56
  1378.0 10.7 all-reduce.6.cloned.1.call-done
  1389.8 4.6 fusion.10
  1394.4 13.3 bitcast_add_fusion
  1409.4 3.9 fusion.7
  1413.4 13.3 copy.43
  1426.7 30.0 %gather_fusion = f32[128,16,256]{1,0,2:T(8,128)} fusion(f32[128,16,384]{1,0,2:T(8,128)} %copy.43, s32[128]{0:T(128)S(1)} %get-tuple-element.65), kind=kCustom, calls=%fused_computation | custom fusion | bytes 4195840 | tf_op jit(solution)/shard_map/vmap()/gather | solution.py:38
  1456.6 9.6 copy.44
  (637 shorter events, 1047.5 us)
Async XLA Ops:
  6.5 1382.1 %all-reduce.6.cloned.1.call-start = ((), (), s32[]{:S(2)}) async-start(), calls=%async_computation | async-start | bytes 393216 | tf_op jit(solution)/shard_map/psum | solution.py:88
  14.0 3.1 copy-start.4
  1164.7 13.7 slice-start
  1164.7 13.7 slice-start.1
  1170.0 139.6 %collective-permute-start = (f32[2,128,16,192]{1,3,2,0:T(8,128)S(1)}, f32[2,128,16,192]{1,3,2,0:T(8,128)}, u32[]{:S(2)}, u32[]{:S(2)}) collective-permute-start(f32[2,128,16,192]{1,3,2,0:T(8,128)S(1)} %get-tuple-element.75), channel_id=1, source_target_pairs={{0,4},{4,8},{8,12},{12,16},{16,20},{20,24},{24,28},{1,5},{5,9},{9,... | collective-permute-start | bytes 9437192 | tf_op jit(solution)/shard_map/ppermute | solution.py:19
  1176.5 6.5 copy-start.5
  1176.5 138.3 %collective-permute-start.1 = (f32[2,128,16,192]{1,3,2,0:T(8,128)}, f32[2,128,16,192]{1,3,2,0:T(8,128)S(1)}, u32[]{:S(2)}, u32[]{:S(2)}) collective-permute-start(f32[2,128,16,192]{1,3,2,0:T(8,128)} %get-tuple-element.76), channel_id=1, source_target_pairs={{4,0},{8,4},{12,8},{16,12},{20,16},{24,20},{28,24},{5,1},{9,5},{13... | collective-permute-start | bytes 9437192 | tf_op jit(solution)/shard_map/ppermute | solution.py:19
  1324.7 9.3 copy-start
  1337.6 4.7 copy-start.2
  1344.8 4.7 copy-start.1
  1374.3 14.4 copy-start.3
Sparse Core Ops, SparseCore 0:
  1355.6 33.0 all-reduce.5
where the time goes:
time: 1510 us; the launch traced here: 1480 us
  other arithmetic  690 us (46%)
  local copies, waits for them, and re-layouts  589 us (39%)
  waiting for transfers between devices  137 us (9%)
  matrix products  36.4 us (2%)
    scatter x256, other arithmetic  681 us
    scatter x384, local copies, waits for them, and re-layouts  460 us
    ppermute x2, waiting for transfers between devices, passed_along(): lax.ppermute(value, axis, [(source, source + steps) for source in range(f...  127 us
    gather x2, local copies, waits for them, and re-layouts, pick_row(): lax.dynamic_slice(window_row, (jnp.int32(0), column_shift), (window_row.s...  39.5 us
  transfers between devices with their start and end apart: 3, of which 2 were waited for; matrix products, arithmetic and copies ran while one was open for 2% of the time, Pallas kernels for 0%

commit v1 on v0

v1 whole, which is shorter than its diff:
```python
import functools
import math

import jax
import jax.numpy as jnp
from jax import lax
from jax.experimental import pallas as pl
from jax.experimental.pallas import tpu as pltpu
from jax.sharding import PartitionSpec as P


BLOCK_FUNCTIONS = 128
PATCH = 256
SPREAD = 128
REACH = 1
BSTEP = 192
SEG = 16384
LANES = 128
HALF = LANES // 2
ROWS = 32
TILES = (PATCH + SPREAD) // LANES
SLOTS = 2 * REACH + 1
WIDE = SLOTS * BLOCK_FUNCTIONS
PAIR = 2
OUTSIDE = 1 << 16
NT = (((1,), (1,)), ((), ()))


def bounds_of(planes, edges):
    marks = sorted({edge * planes // 16 // PAIR * PAIR for edge in edges})
    return list(zip(marks[:-1], marks[1:]))


def turned(values, index):
    return jnp.take_along_axis(values, index, axis=1)


def lane_of(rows=ROWS):
    return lax.broadcasted_iota(jnp.int32, (rows, LANES), 1)


def row_groups():
    return [slice(start, start + ROWS) for start in range(0, BLOCK_FUNCTIONS, ROWS)]


def halves(values):
    high = values.astype(jnp.bfloat16)
    return high, (values - high.astype(jnp.float32)).astype(jnp.bfloat16)


def pack_kernel(me_ref, box_ref, a_ref, b_ref):
    odd = me_ref[0] % 2
    for rows in row_groups():
        low = lane_of() < HALF
        split = []
        for plane in range(PAIR):
            whole_at = pl.multiple_of(plane * PATCH + odd * LANES, LANES)
            split_at = pl.multiple_of(plane * PATCH + (1 - odd) * LANES, LANES)
            a_ref[rows, plane * LANES : (plane + 1) * LANES] = box_ref[0, rows, pl.ds(whole_at, LANES)]
            split.append(box_ref[0, rows, pl.ds(split_at, LANES)])
        left = jnp.where(low, split[0], pltpu.roll(split[1], HALF, 1))
        right = jnp.where(low, pltpu.roll(split[0], HALF, 1), split[1])
        a_ref[rows, PAIR * LANES : TILES * LANES] = jnp.where(odd == 1, right, left)
        b_ref[rows, :] = jnp.where(odd == 1, left, right)


def packed(me, orbitals, member, start, stop):
    pairs_in = (stop - start) // PAIR
    first = start // PAIR
    return pl.pallas_call(
        pack_kernel,
        grid=(pairs_in,),
        in_specs=[
            pl.BlockSpec(memory_space=pltpu.SMEM),
            pl.BlockSpec((1, BLOCK_FUNCTIONS, PAIR * PATCH), lambda i: (member, 0, first + i)),
        ],
        out_specs=[
            pl.BlockSpec((BLOCK_FUNCTIONS, TILES * LANES), lambda i: (0, i)),
            pl.BlockSpec((BLOCK_FUNCTIONS, LANES), lambda i: (0, i)),
        ],
        out_shape=[
            jax.ShapeDtypeStruct((BLOCK_FUNCTIONS, pairs_in * TILES * LANES), jnp.float32),
            jax.ShapeDtypeStruct((BLOCK_FUNCTIONS, pairs_in * LANES), jnp.float32),
        ],
        cost_estimate=pl.CostEstimate(
            flops=0, bytes_accessed=8 * BLOCK_FUNCTIONS * pairs_in * PAIR * PATCH, transcendentals=0
        ),
        compiler_params=pltpu.CompilerParams(vmem_limit_bytes=60 << 20),
        name="pack",
    )(me, orbitals)


def make_tables(groups, me, offsets_ref, table_ref):
    upward = 1 - 2 * (me % 2)
    for source, sign in enumerate((0, upward, -upward)):
        block = me + sign
        row = jnp.clip(block, 0, groups - 1)
        shift = jnp.clip(offsets_ref[pl.ds(row, 1), :] - BSTEP * row, 0, SPREAD)
        if source > 0:
            shift = shift + jnp.where(sign > 0, BSTEP - LANES, -BSTEP)
            shift = shift + jnp.where(block == row, 0, OUTSIDE)
        table_ref[source] = jnp.broadcast_to(shift, (BLOCK_FUNCTIONS, LANES)).T


def own_tiles(table_ref, rows, first, second):
    ahead = lane_of() - table_ref[0, rows, :]
    index, inside = ahead & (LANES - 1), ahead >= 0
    left, right = turned(first, index), turned(second, index)
    zero = jnp.zeros_like(left)
    return jnp.where(inside, left, zero), jnp.where(inside, right, left), jnp.where(inside, zero, right)


def near_tiles(table_ref, source, rows, fixed, a_ref, b_ref):
    ahead = lane_of() - table_ref[source, rows, :]
    index = ahead & (LANES - 1)
    tile_of = ahead >> 7
    fixed_in = tile_of - fixed
    split_in = tile_of - (1 - fixed)
    within = index & (HALF - 1)
    shared = a_ref[rows, PAIR * LANES : TILES * LANES]
    result = []
    for plane in range(PAIR):
        whole = turned(a_ref[rows, plane * LANES : (plane + 1) * LANES], index)
        split = turned(shared, within + plane * HALF)
        if b_ref is not None:
            split = jnp.where((index >> 6) == fixed, split, turned(b_ref[rows, :], within + plane * HALF))
        zero = jnp.zeros_like(whole)
        result.append(
            tuple(
                jnp.where(fixed_in == -at, whole, jnp.where(split_in == -at, split, zero))
                for at in range(2)
            )
        )
    return result


def place_all(table_ref, odd, member, own_ref, ya_ref, yb_ref, za_ref, hi_ref, lo_ref):
    y_slot, z_slot = 2 * (1 - odd), 2 * odd
    for rows in row_groups():
        for plane in range(PAIR):
            lanes = slice(plane * LANES, (plane + 1) * LANES)
            cut = plane * PATCH
            tiles = own_tiles(
                table_ref, rows, own_ref[member, rows, cut : cut + LANES],
                own_ref[member, rows, cut + LANES : cut + PATCH],
            )
            stack = slice(BLOCK_FUNCTIONS + rows.start, BLOCK_FUNCTIONS + rows.stop)
            for k in range(TILES):
                hi_ref[k, stack, lanes], lo_ref[k, stack, lanes] = halves(tiles[k])
        for source, slot, a_ref, b_ref in ((1, y_slot, ya_ref, yb_ref), (2, z_slot, za_ref, None)):
            base = pl.multiple_of(slot * BLOCK_FUNCTIONS + rows.start, ROWS)
            first = slot // 2
            for plane, tiles in enumerate(near_tiles(table_ref, source, rows, 1 - odd, a_ref, b_ref)):
                lanes = slice(plane * LANES, (plane + 1) * LANES)
                for at in range(2):
                    high, low = halves(tiles[at])
                    hi_ref[first + at, pl.ds(base, ROWS), lanes] = high
                    lo_ref[first + at, pl.ds(base, ROWS), lanes] = low


def slots_of(k):
    start, stop = (0 if k < 2 else 1), (2 if k < 1 else 3)
    return slice(start * BLOCK_FUNCTIONS, stop * BLOCK_FUNCTIONS)


def mixed(m_hi, m_lo, s_hi, s_lo, k):
    part = slots_of(k)
    dot = functools.partial(jnp.dot, preferred_element_type=jnp.float32)
    return dot(m_hi[:, part], s_hi[k, part, :]) + (
        dot(m_hi[:, part], s_lo[k, part, :]) + dot(m_lo[:, part], s_hi[k, part, :])
    )


def gram_kernel(
    groups, me_ref, pairs_ref, offsets_ref, kernel_ref, own_ref, ya_ref, yb_ref, za_ref, before_ref,
    out_ref, sum_ref, table_ref, m_hi, m_lo, l_hi, l_lo, r_hi, r_lo,
):
    me = me_ref[0]

    @pl.when(pl.program_id(0) == 0)
    def _():
        make_tables(groups, me, offsets_ref, table_ref)
        for slot in range(SLOTS):
            part = slice(slot * BLOCK_FUNCTIONS, (slot + 1) * BLOCK_FUNCTIONS)
            m_hi[:, part], m_lo[:, part] = halves(kernel_ref[0, slot] * pairs_ref[0, slot].astype(jnp.float32))
        out_ref[...] = before_ref[...]

    for rows in row_groups():
        for plane in range(PAIR):
            lanes = slice(plane * LANES, (plane + 1) * LANES)
            cut = plane * PATCH
            tiles = own_tiles(
                table_ref, rows, own_ref[0, rows, cut : cut + LANES],
                own_ref[0, rows, cut + LANES : cut + PATCH],
            )
            for k in range(TILES):
                l_hi[k, rows, lanes], l_lo[k, rows, lanes] = halves(tiles[k])
    place_all(table_ref, me % 2, 1, own_ref, ya_ref, yb_ref, za_ref, r_hi, r_lo)
    dot = functools.partial(lax.dot_general, dimension_numbers=NT, preferred_element_type=jnp.float32)
    for k in range(TILES):
        part = slots_of(k)
        out_ref[:, part] += dot(l_hi[k], r_hi[k, part, :]) + (
            dot(l_hi[k], r_lo[k, part, :]) + dot(l_lo[k], r_hi[k, part, :])
        )
        sum_ref[:, k * PAIR * LANES : (k + 1) * PAIR * LANES] = mixed(m_hi, m_lo, r_hi, r_lo, k)


def apply_kernel(
    groups, volume, me_ref, pairs_ref, offsets_ref, near_ref, far_ref, own_ref, ya_ref, yb_ref, za_ref, sum_ref,
    *rest,
):
    out_ref, table_ref, m_hi, m_lo, s_hi, s_lo, acc_ref = rest[-7:]
    me = me_ref[0]

    @pl.when(pl.program_id(0) == 0)
    def _():
        make_tables(groups, me, offsets_ref, table_ref)
        for slot in range(SLOTS):
            part = slice(slot * BLOCK_FUNCTIONS, (slot + 1) * BLOCK_FUNCTIONS)
            weight = -volume * pairs_ref[0, slot].astype(jnp.float32)
            m_hi[:, part], m_lo[:, part] = halves((near_ref[:, part] + far_ref[:, part]) * weight)

    place_all(table_ref, me % 2, 0, own_ref, ya_ref, yb_ref, za_ref, s_hi, s_lo)
    for k in range(TILES):
        lanes = slice(k * PAIR * LANES, (k + 1) * PAIR * LANES)
        acc_ref[k] = sum_ref[:, lanes] + mixed(m_hi, m_lo, s_hi, s_lo, k)
    for rows in row_groups():
        beyond = lane_of() + table_ref[0, rows, :]
        index, inside = beyond & (LANES - 1), beyond < LANES
        for plane in range(PAIR):
            lanes = slice(plane * LANES, (plane + 1) * LANES)
            a, b, c = (turned(acc_ref[k, rows, lanes], index) for k in range(TILES))
            out_ref[rows, plane * PATCH : plane * PATCH + LANES] = jnp.where(inside, a, b)
            out_ref[rows, plane * PATCH + LANES : (plane + 1) * PATCH] = jnp.where(inside, b, c)


def whole(shape):
    return pl.BlockSpec(shape, lambda i: (0,) * len(shape))


SMEM = pl.BlockSpec(memory_space=pltpu.SMEM)
TABLES = pltpu.VMEM((3, BLOCK_FUNCTIONS, LANES), jnp.int32)


def stacks(depth):
    return [pltpu.VMEM((TILES, depth, PAIR * LANES), jnp.bfloat16)] * 2


def gram(me, pairs, offsets, kernel, orbitals, ya, yb, za, before, start, stop):
    first, steps = start // PAIR, (stop - start) // PAIR
    lanes = TILES * PAIR * LANES
    return pl.pallas_call(
        functools.partial(gram_kernel, offsets.shape[0]),
        grid=(steps,),
        in_specs=[
            SMEM, SMEM, whole(offsets.shape), whole(kernel.shape),
            pl.BlockSpec((2, BLOCK_FUNCTIONS, PAIR * PATCH), lambda i: (0, 0, first + i)),
            pl.BlockSpec((BLOCK_FUNCTIONS, TILES * LANES), lambda i: (0, i)),
            pl.BlockSpec((BLOCK_FUNCTIONS, LANES), lambda i: (0, i)),
            pl.BlockSpec((BLOCK_FUNCTIONS, TILES * LANES), lambda i: (0, i)),
            whole(before.shape),
        ],
        out_specs=[whole(before.shape), pl.BlockSpec((BLOCK_FUNCTIONS, lanes), lambda i: (0, i))],
        out_shape=[
            jax.ShapeDtypeStruct(before.shape, jnp.float32),
            jax.ShapeDtypeStruct((BLOCK_FUNCTIONS, steps * lanes), jnp.float32),
        ],
        scratch_shapes=[TABLES]
        + [pltpu.VMEM((BLOCK_FUNCTIONS, WIDE), jnp.bfloat16)] * 2
        + stacks(BLOCK_FUNCTIONS) + stacks(WIDE),
        cost_estimate=pl.CostEstimate(
            flops=12 * steps * BLOCK_FUNCTIONS * WIDE * lanes,
            bytes_accessed=4 * BLOCK_FUNCTIONS * steps * (4 * PAIR * PATCH + lanes),
            transcendentals=0,
        ),
        compiler_params=pltpu.CompilerParams(vmem_limit_bytes=16 << 20),
        name="gram",
    )(me, pairs, offsets, kernel, orbitals, ya, yb, za, before)


def applied(me, pairs, offsets, near, far, orbitals, ya, yb, za, sums, skip, held, start, stop):
    first, steps = start // PAIR, (stop - start) // PAIR
    behind = (start - skip) // PAIR
    lanes = TILES * PAIR * LANES
    operands = [me, pairs, offsets, near, far, orbitals, ya, yb, za, sums]
    in_specs = [
        SMEM, SMEM, whole(offsets.shape), whole(near.shape), whole(far.shape),
        pl.BlockSpec((1, BLOCK_FUNCTIONS, PAIR * PATCH), lambda i: (0, 0, first + i)),
        pl.BlockSpec((BLOCK_FUNCTIONS, TILES * LANES), lambda i: (0, i)),
        pl.BlockSpec((BLOCK_FUNCTIONS, LANES), lambda i: (0, i)),
        pl.BlockSpec((BLOCK_FUNCTIONS, TILES * LANES), lambda i: (0, i)),
        pl.BlockSpec((BLOCK_FUNCTIONS, lanes), lambda i: (0, behind + i)),
    ]
    aliases = {}
    if held is not None:
        aliases = {len(operands): 0}
        operands.append(held)
        in_specs.append(pl.BlockSpec(memory_space=pl.ANY))
    return pl.pallas_call(
        functools.partial(apply_kernel, offsets.shape[0], 1.0 / math.sqrt(SEG)),
        grid=(steps,),
        in_specs=in_specs,
        out_specs=pl.BlockSpec((BLOCK_FUNCTIONS, PAIR * PATCH), lambda i: (0, first + i)),
        out_shape=jax.ShapeDtypeStruct(orbitals.shape[1:], jnp.float32),
        input_output_aliases=aliases,
        scratch_shapes=[TABLES]
        + [pltpu.VMEM((BLOCK_FUNCTIONS, WIDE), jnp.bfloat16)] * 2
        + stacks(WIDE)
        + [pltpu.VMEM((TILES, BLOCK_FUNCTIONS, PAIR * LANES), jnp.float32)],
        cost_estimate=pl.CostEstimate(
            flops=6 * steps * BLOCK_FUNCTIONS * WIDE * lanes,
            bytes_accessed=4 * BLOCK_FUNCTIONS * steps * (4 * PAIR * PATCH + lanes),
            transcendentals=0,
        ),
        compiler_params=pltpu.CompilerParams(vmem_limit_bytes=16 << 20),
        name="apply",
    )(*operands)


FIRST_EDGES = (0, 6, 10, 16)
SECOND_EDGES = (0, 6, 10, 14, 16)


def per_device(orbitals, offsets, pairs, kernel):
    per_dev, planes = orbitals.shape[1], orbitals.shape[2] // PATCH
    groups, slabs = lax.axis_size("orb"), lax.axis_size("slab")
    assert per_dev == BLOCK_FUNCTIONS and groups % 2 == 0
    assert planes % PAIR == 0 and slabs & (slabs - 1) == 0
    me = lax.axis_index("orb").astype(jnp.int32)[None]
    offsets = offsets.reshape(groups, per_dev)

    swap = [(at, at ^ 1) for at in range(groups)]
    onward = [(at, (at + 2 - 4 * (at % 2)) % groups) for at in range(groups)]
    bounds = {1: bounds_of(planes, FIRST_EDGES), 0: bounds_of(planes, SECOND_EDGES)}

    ya, yb, za = {}, {}, {}
    for member in (1, 0):
        for number, (start, stop) in enumerate(bounds[member]):
            a, b = packed(me, orbitals, member, start, stop)
            ya[member, number] = lax.ppermute(a, "orb", swap)
            yb[member, number] = lax.ppermute(b, "orb", swap)
            za[member, number] = lax.ppermute(ya[member, number], "orb", onward)

    total, sums = jnp.zeros((per_dev, WIDE), jnp.float32), []
    for number, (start, stop) in enumerate(bounds[1]):
        parts = (ya[1, number], yb[1, number], za[1, number])
        total, part = gram(me, pairs, offsets, kernel, orbitals, *parts, total, start, stop)
        sums.append(part)
    far, step = jnp.zeros_like(total), 1
    while step < slabs:
        if step > 1:
            total = total + far
        far = lax.ppermute(total, "slab", [(at, at ^ step) for at in range(slabs)])
        step *= 2

    held = None
    for number, (start, stop) in enumerate(bounds[0]):
        [inside] = [at for at, (low, high) in enumerate(bounds[1]) if low <= start and stop <= high]
        parts = (ya[0, number], yb[0, number], za[0, number])
        held = applied(
            me, pairs, offsets, total, far, orbitals, *parts, sums[inside], bounds[1][inside][0],
            held, start, stop,
        )
    return held


def solution(mesh):
    placed = (P(None, "orb", "slab"), P(), P("orb", None), P("orb", None, None, None))
    return jax.shard_map(per_device, mesh=mesh, in_specs=placed, out_specs=P("orb", "slab"), check_vma=False)
```

time: 1510 us -> 123 us (0.08); the launches traced: 1480 us -> 122 us
  other arithmetic: 690 us -> 0.96 us
  local copies, waits for them, and re-layouts: 589 us -> 4.42 us
  waiting for transfers between devices: 137 us -> 33.3 us
  Pallas kernels: 0 us -> 50.1 us
  matrix products: 36.4 us -> 0 us
  starting transfers between devices: 8.39 us -> 33.4 us
    scatter x257 -> x0, other arithmetic: 681 us -> none
    scatter x386 -> x0, local copies, waits for them, and re-layouts: 471 us -> none
    ppermute x2 -> x23, waiting for transfers between devices: 127 us -> 33.3 us  [the longest x7 20.1 us: per_device(): ya[member, number] = lax.ppermute(a, 'orb', swap)]
    pallas_call x0 -> x14, Pallas kernels: none -> 50.1 us  [the longest x4 17.1 us: applied(): pl.pallas_call(functools.partial(apply_kernel, offsets.shape[0], 1.0 / ma...]
    gather x2 -> x0, local copies, waits for them, and re-layouts: 39.5 us -> none  [pick_row(): lax.dynamic_slice(window_row, (jnp.int32(0), column_shift), (window_row.s...]
    dot_general x6 -> x0, matrix products: 36.4 us -> none  [the longest x3 21.9 us: per_device(): jnp.einsum('bmij,mbjxc->bixc', both_rows, nearby[..., source], precision=...]
    ppermute x2 -> x23, starting transfers between devices: 8.39 us -> 33.4 us  [the longest x7 13 us: per_device(): yb[member, number] = lax.ppermute(b, 'orb', swap)]
    unnamed x23 -> x22, local copies, waits for them, and re-layouts: 25.9 us -> 4.41 us
  transfers between devices with their start and end apart: 3 -> 23, of which waited for: 2 -> 7; matrix products, arithmetic and copies ran while one was open for 2% -> 1% of each run, Pallas kernels for 0% -> 36%
where the time goes in v1:
time: 123 us; the launch traced here: 122 us
  Pallas kernels  50.1 us (41%)
  starting transfers between devices  33.4 us (27%)
  waiting for transfers between devices  33.3 us (27%)
  local copies, waits for them, and re-layouts  4.42 us (4%)
    ppermute x7, waiting for transfers between devices, per_device(): ya[member, number] = lax.ppermute(a, 'orb', swap)  20.1 us
    pallas_call x4, Pallas kernels, applied(): pl.pallas_call(functools.partial(apply_kernel, offsets.shape[0], 1.0 / ma...  17.1 us
    pallas_call x7, Pallas kernels, packed(): pl.pallas_call(pack_kernel, grid=(pairs_in,), in_specs=[pl.BlockSpec(memo...  16.8 us
    pallas_call x3, Pallas kernels, gram(): pl.pallas_call(functools.partial(gram_kernel, offsets.shape[0]), grid=(st...  16.1 us
    ppermute x7, starting transfers between devices, per_device(): yb[member, number] = lax.ppermute(b, 'orb', swap)  13 us
    ppermute x7, waiting for transfers between devices, per_device(): yb[member, number] = lax.ppermute(b, 'orb', swap)  12.8 us
    ppermute x7, starting transfers between devices, per_device(): ya[member, number] = lax.ppermute(a, 'orb', swap)  10.1 us
    ppermute x7, starting transfers between devices, per_device(): za[member, number] = lax.ppermute(ya[member, number], 'orb', onward)  8.78 us
  transfers between devices with their start and end apart: 23, of which 7 were waited for; matrix products, arithmetic and copies ran while one was open for 1% of the time, Pallas kernels for 36%

profile of v1, /device:TPU:0, one launch (start us, length us, event | category | flops | bytes accessed | tf_op | source)
XLA Modules:
  0.0 122.3 jit_solution(11074136332543895707)
XLA Ops:
  0.0 3.0 %pack.9 = (f32[128,1152]{1,0:T(8,128)}, f32[128,384]{1,0:T(8,128)}) custom-call(s32[1]{0:T(128)} %bitcast.me_ref, f32[2,128,4096]{2,1,0:T(8,128)} %own_ref.13), custom_call_target="tpu_custom_call" | custom-call | bytes 1572864 | tf_op jit(solution)/shard_map/pack/pallas_call | solution.py:70
  3.0 3.0 %collective-permute-start.6 = (f32[128,1152]{1,0:T(8,128)}, f32[128,1152]{1,0:T(8,128)S(1)}, u32[]{:S(2)}, u32[]{:S(2)}) collective-permute-start(f32[128,1152]{1,0:T(8,128)} %get-tuple-element.29), channel_id=1, source_target_pairs={{0,4},{4,0},{8,12},{12,8},{16,20},{20,16},{24,28},{28,24},{1,5},{5... | collective-permute-start | bytes 1769480 | tf_op jit(solution)/shard_map/ppermute | solution.py:340
  6.0 3.0 %pack.7 = (f32[128,1152]{1,0:T(8,128)}, f32[128,384]{1,0:T(8,128)}) custom-call(s32[1]{0:T(128)} %bitcast.me_ref, f32[2,128,4096]{2,1,0:T(8,128)} %own_ref.13), custom_call_target="tpu_custom_call" | custom-call | bytes 1572864 | tf_op jit(solution)/shard_map/pack/pallas_call | solution.py:70
  9.0 0.0 collective-permute-start
  9.0 2.0 %pack.8 = (f32[128,768]{1,0:T(8,128)}, f32[128,256]{1,0:T(8,128)}) custom-call(s32[1]{0:T(128)} %bitcast.me_ref, f32[2,128,4096]{2,1,0:T(8,128)} %own_ref.13), custom_call_target="tpu_custom_call" | custom-call | bytes 1048576 | tf_op jit(solution)/shard_map/pack/pallas_call | solution.py:70
  11.0 2.1 %collective-permute-start.3 = (f32[128,768]{1,0:T(8,128)}, f32[128,768]{1,0:T(8,128)}, u32[]{:S(2)}, u32[]{:S(2)}) collective-permute-start(f32[128,768]{1,0:T(8,128)} %get-tuple-element.27), channel_id=1, source_target_pairs={{0,4},{4,0},{8,12},{12,8},{16,20},{20,16},{24,28},{28,24},{1,5},{5... | collective-permute-start | bytes 1179656 | tf_op jit(solution)/shard_map/ppermute | solution.py:340
  13.1 3.1 %pack.13 = (f32[128,1152]{1,0:T(8,128)}, f32[128,384]{1,0:T(8,128)}) custom-call(s32[1]{0:T(128)} %bitcast.me_ref, f32[2,128,4096]{2,1,0:T(8,128)} %own_ref.13), custom_call_target="tpu_custom_call" | custom-call | bytes 1572864 | tf_op jit(solution)/shard_map/pack/pallas_call | solution.py:70
  16.1 0.1 collective-permute-start.20
  16.2 4.2 %collective-permute-done.6.ya_ref = f32[128,1152]{1,0:T(8,128)S(1)} collective-permute-done((f32[128,1152]{1,0:T(8,128)}, f32[128,1152]{1,0:T(8,128)S(1)}, u32[]{:S(2)}, u32[]{:S(2)}) %collective-permute-start.6) | collective-permute-done | bytes 589856 | tf_op jit(solution)/shard_map/ppermute | solution.py:340
  20.4 2.1 %collective-permute-start.8 = (f32[128,1152]{1,0:T(8,128)S(1)}, f32[128,1152]{1,0:T(8,128)S(1)}, u32[]{:S(2)}, u32[]{:S(2)}) collective-permute-start(f32[128,1152]{1,0:T(8,128)S(1)} %collective-permute-done.6.ya_ref), channel_id=1, source_target_pairs={{0,8},{4,28},{8,16},{12,4},{16,24},{20,12},{24,0},{28,20},{1,9},{5... | collective-permute-start | bytes 1769480 | tf_op jit(solution)/shard_map/ppermute | solution.py:342
  22.5 10.6 %collective-permute-done.ya_ref = f32[128,1152]{1,0:T(8,128)S(1)} collective-permute-done((f32[128,1152]{1,0:T(8,128)}, f32[128,1152]{1,0:T(8,128)S(1)}, u32[]{:S(2)}, u32[]{:S(2)}) %collective-permute-start) | collective-permute-done | bytes 589856 | tf_op jit(solution)/shard_map/ppermute | solution.py:340
  33.0 2.1 %collective-permute-start.2 = (f32[128,1152]{1,0:T(8,128)S(1)}, f32[128,1152]{1,0:T(8,128)}, u32[]{:S(2)}, u32[]{:S(2)}) collective-permute-start(f32[128,1152]{1,0:T(8,128)S(1)} %collective-permute-done.ya_ref), channel_id=1, source_target_pairs={{0,8},{4,28},{8,16},{12,4},{16,24},{20,12},{24,0},{28,20},{1,9},{5... | collective-permute-start | bytes 1769480 | tf_op jit(solution)/shard_map/ppermute | solution.py:342
  35.1 3.5 %collective-permute-start.4 = (f32[128,256]{1,0:T(8,128)S(1)}, f32[128,256]{1,0:T(8,128)S(1)}, u32[]{:S(2)}, u32[]{:S(2)}) collective-permute-start(f32[128,256]{1,0:T(8,128)S(1)} %copy-done.9), channel_id=1, source_target_pairs={{0,4},{4,0},{8,12},{12,8},{16,20},{20,16},{24,28},{28,24},{1,5},{5... | collective-permute-start | bytes 393224 | tf_op jit(solution)/shard_map/ppermute | solution.py:341
  38.7 2.9 %collective-permute-done.3.ya_ref = f32[128,768]{1,0:T(8,128)} collective-permute-done((f32[128,768]{1,0:T(8,128)}, f32[128,768]{1,0:T(8,128)}, u32[]{:S(2)}, u32[]{:S(2)}) %collective-permute-start.3) | collective-permute-done | bytes 393248 | tf_op jit(solution)/shard_map/ppermute | solution.py:340
  41.6 2.1 %collective-permute-start.5 = (f32[128,768]{1,0:T(8,128)}, f32[128,768]{1,0:T(8,128)}, u32[]{:S(2)}, u32[]{:S(2)}) collective-permute-start(f32[128,768]{1,0:T(8,128)} %collective-permute-done.3.ya_ref), channel_id=1, source_target_pairs={{0,8},{4,28},{8,16},{12,4},{16,24},{20,12},{24,0},{28,20},{1,9},{5... | collective-permute-start | bytes 1179656 | tf_op jit(solution)/shard_map/ppermute | solution.py:342
  43.7 12.4 %collective-permute-done.4.yb_ref = f32[128,256]{1,0:T(8,128)S(1)} collective-permute-done((f32[128,256]{1,0:T(8,128)S(1)}, f32[128,256]{1,0:T(8,128)S(1)}, u32[]{:S(2)}, u32[]{:S(2)}) %collective-permute-start.4) | collective-permute-done | bytes 131104 | tf_op jit(solution)/shard_map/ppermute | solution.py:341
  56.1 1.7 %collective-permute-start.7 = (f32[128,384]{1,0:T(8,128)S(1)}, f32[128,384]{1,0:T(8,128)S(1)}, u32[]{:S(2)}, u32[]{:S(2)}) collective-permute-start(f32[128,384]{1,0:T(8,128)S(1)} %copy-done.7), channel_id=1, source_target_pairs={{0,4},{4,0},{8,12},{12,8},{16,20},{20,16},{24,28},{28,24},{1,5},{5... | collective-permute-start | bytes 589832 | tf_op jit(solution)/shard_map/ppermute | solution.py:341
  57.8 1.9 %pack.12 = (f32[128,768]{1,0:T(8,128)}, f32[128,256]{1,0:T(8,128)}) custom-call(s32[1]{0:T(128)} %bitcast.me_ref, f32[2,128,4096]{2,1,0:T(8,128)} %own_ref.13), custom_call_target="tpu_custom_call" | custom-call | bytes 1048576 | tf_op jit(solution)/shard_map/pack/pallas_call | solution.py:70
  59.8 0.0 copy-start.6
  59.8 2.0 %pack.11 = (f32[128,768]{1,0:T(8,128)}, f32[128,256]{1,0:T(8,128)}) custom-call(s32[1]{0:T(128)} %bitcast.me_ref, f32[2,128,4096]{2,1,0:T(8,128)} %own_ref.13), custom_call_target="tpu_custom_call" | custom-call | bytes 1048576 | tf_op jit(solution)/shard_map/pack/pallas_call | solution.py:70
  61.8 0.4 collective-permute-done.7.yb_ref
  62.2 1.4 %collective-permute-start.1 = (f32[128,384]{1,0:T(8,128)}, f32[128,384]{1,0:T(8,128)S(1)}, u32[]{:S(2)}, u32[]{:S(2)}) collective-permute-start(f32[128,384]{1,0:T(8,128)} %get-tuple-element.26), channel_id=1, source_target_pairs={{0,4},{4,0},{8,12},{12,8},{16,20},{20,16},{24,28},{28,24},{1,5},{5... | collective-permute-start | bytes 589832 | tf_op jit(solution)/shard_map/ppermute | solution.py:341
  63.6 0.0 collective-permute-done.20.ya_ref
  63.6 0.7 collective-permute-start.17
  64.3 0.0 collective-permute-done.8.za_ref
  64.3 1.4 %collective-permute-start.14 = (f32[128,768]{1,0:T(8,128)}, f32[128,768]{1,0:T(8,128)}, u32[]{:S(2)}, u32[]{:S(2)}) collective-permute-start(f32[128,768]{1,0:T(8,128)} %get-tuple-element.37), channel_id=1, source_target_pairs={{0,4},{4,0},{8,12},{12,8},{16,20},{20,16},{24,28},{28,24},{1,5},{5... | collective-permute-start | bytes 1179656 | tf_op jit(solution)/shard_map/ppermute | solution.py:340
  65.7 0.0 copy-start
  65.7 2.2 %copy-done = f32[2,128,4096]{2,1,0:T(8,128)S(1)} copy-done((f32[2,128,4096]{2,1,0:T(8,128)S(1)}, f32[2,128,4096]{2,1,0:T(8,128)}, u32[]{:S(2)}) %copy-start) | copy-done | bytes 4194328
  67.9 5.4 %gram.3 = (f32[128,384]{1,0:T(8,128)S(1)}, f32[128,2304]{1,0:T(8,128)S(1)}) custom-call(s32[1]{0:T(128)} %bitcast.me_ref, s32[1,3]{1,0:T(1,128)S(1)} %copy-done.6, s32[8,128]{1,0:T(8,128)S(1)} %bitcast.2, f32[1,3,128,128]{3,2,1,0:T(8,128)S(1)} %copy-done.2, f32[2,128,4096]{2,1,0:T(8,128)S(1)} %copy-done, f32[128,1152]{1,0:T(8,128)S(1)} %collective-permute-done.6.ya_ref, ...), custom_call_target="tpu_custom_call" | custom-call | flops 1358954496 | bytes 4325376 | tf_op jit(solution)/shard_map/gram/pallas_call | solution.py:252
  73.3 0.0 collective-permute-done.5.za_ref
  73.3 1.6 %collective-permute-start.22 = (f32[128,1152]{1,0:T(8,128)S(1)}, f32[128,1152]{1,0:T(8,128)}, u32[]{:S(2)}, u32[]{:S(2)}) collective-permute-start(f32[128,1152]{1,0:T(8,128)S(1)} %collective-permute-done.20.ya_ref), channel_id=1, source_target_pairs={{0,8},{4,28},{8,16},{12,4},{16,24},{20,12},{24,0},{28,20},{1,9},{5... | collective-permute-start | bytes 1769480 | tf_op jit(solution)/shard_map/ppermute | solution.py:342
  74.9 4.3 %gram.4 = (f32[128,384]{1,0:T(8,128)S(1)}, f32[128,1536]{1,0:T(8,128)S(1)}) custom-call(s32[1]{0:T(128)} %bitcast.me_ref, s32[1,3]{1,0:T(1,128)S(1)} %copy-done.6, s32[8,128]{1,0:T(8,128)S(1)} %bitcast.3, f32[1,3,128,128]{3,2,1,0:T(8,128)S(1)} %copy-done.2, f32[2,128,4096]{2,1,0:T(8,128)S(1)} %copy-done, f32[128,768]{1,0:T(8,128)} %collective-permute-done.3.ya_ref, ...), custom_call_target="tpu_custom_call" | custom-call | flops 905969664 | bytes 2883584 | tf_op jit(solution)/shard_map/gram/pallas_call | solution.py:252
  79.3 0.0 collective-permute-done.1.yb_ref
  79.3 0.0 collective-permute-done.2.za_ref
  79.3 6.4 %gram.5 = (f32[128,384]{1,0:T(8,128)}, f32[128,2304]{1,0:T(8,128)S(1)}) custom-call(s32[1]{0:T(128)} %bitcast.me_ref, s32[1,3]{1,0:T(1,128)S(1)} %copy-done.6, s32[8,128]{1,0:T(8,128)S(1)} %bitcast.4, f32[1,3,128,128]{3,2,1,0:T(8,128)S(1)} %copy-done.2, f32[2,128,4096]{2,1,0:T(8,128)S(1)} %copy-done, f32[128,1152]{1,0:T(8,128)S(1)} %copy-done.4, ...), custom_call_target="tpu_custom_call" | custom-call | flops 1358954496 | bytes 4325376 | tf_op jit(solution)/shard_map/gram/pallas_call | solution.py:252
  85.7 0.0 collective-permute-start.9
  85.7 2.5 %collective-permute-start.21 = (f32[128,384]{1,0:T(8,128)}, f32[128,384]{1,0:T(8,128)}, u32[]{:S(2)}, u32[]{:S(2)}) collective-permute-start(f32[128,384]{1,0:T(8,128)} %get-tuple-element.43), channel_id=1, source_target_pairs={{0,4},{4,0},{8,12},{12,8},{16,20},{20,16},{24,28},{28,24},{1,5},{5... | collective-permute-start | bytes 589832 | tf_op jit(solution)/shard_map/ppermute | solution.py:341
  88.2 0.0 collective-permute-done.17.ya_ref
  88.2 0.0 collective-permute-start.19
  88.2 0.0 collective-permute-done.14.ya_ref
  88.3 0.8 collective-permute-start.16
  89.0 1.8 %pack.10 = (f32[128,384]{1,0:T(8,128)}, f32[128,128]{1,0:T(8,128)}) custom-call(s32[1]{0:T(128)} %bitcast.me_ref, f32[2,128,4096]{2,1,0:T(8,128)} %own_ref.13), custom_call_target="tpu_custom_call" | custom-call | bytes 524288 | tf_op jit(solution)/shard_map/pack/pallas_call | solution.py:70
  90.8 0.0 collective-permute-done.9
  90.8 2.9 %collective-permute-start.11 = (f32[128,384]{1,0:T(8,128)}, f32[128,384]{1,0:T(8,128)S(1)}, u32[]{:S(2)}, u32[]{:S(2)}) collective-permute-start(f32[128,384]{1,0:T(8,128)} %get-tuple-element.34), channel_id=1, source_target_pairs={{0,4},{4,0},{8,12},{12,8},{16,20},{20,16},{24,28},{28,24},{1,5},{5... | collective-permute-start | bytes 589832 | tf_op jit(solution)/shard_map/ppermute | solution.py:340
  93.7 1.0 add.3.near_ref
  94.6 0.0 collective-permute-done.21.yb_ref
  94.6 1.6 %collective-permute-start.10 = (f32[128,384]{1,0:T(8,128)S(1)}, f32[128,384]{1,0:T(8,128)S(1)}, u32[]{:S(2)}, u32[]{:S(2)}) collective-permute-start(f32[128,384]{1,0:T(8,128)S(1)} %add.3.near_ref), channel_id=1, source_target_pairs={{0,2},{1,3},{2,0},{3,1},{4,6},{5,7},{6,4},{7,5},{8,10},{9,11},{10,... | collective-permute-start | bytes 589832 | tf_op jit(solution)/shard_map/ppermute | solution.py:353
  96.2 2.4 %collective-permute-done.11.ya_ref = f32[128,384]{1,0:T(8,128)S(1)} collective-permute-done((f32[128,384]{1,0:T(8,128)}, f32[128,384]{1,0:T(8,128)S(1)}, u32[]{:S(2)}, u32[]{:S(2)}) %collective-permute-start.11) | collective-permute-done | bytes 196640 | tf_op jit(solution)/shard_map/ppermute | solution.py:340
  98.6 1.7 %collective-permute-start.18 = (f32[128,256]{1,0:T(8,128)}, f32[128,256]{1,0:T(8,128)S(1)}, u32[]{:S(2)}, u32[]{:S(2)}) collective-permute-start(f32[128,256]{1,0:T(8,128)} %get-tuple-element.40), channel_id=1, source_target_pairs={{0,4},{4,0},{8,12},{12,8},{16,20},{20,16},{24,28},{28,24},{1,5},{5... | collective-permute-start | bytes 393224 | tf_op jit(solution)/shard_map/ppermute | solution.py:341
  100.4 0.0 collective-permute-done.22.za_ref
  100.4 0.1 collective-permute-start.13
  100.5 0.4 collective-permute-done.10.far_ref
  100.9 2.0 %collective-permute-start.15 = (f32[128,256]{1,0:T(8,128)S(1)}, f32[128,256]{1,0:T(8,128)S(1)}, u32[]{:S(2)}, u32[]{:S(2)}) collective-permute-start(f32[128,256]{1,0:T(8,128)S(1)} %copy-done.8), channel_id=1, source_target_pairs={{0,4},{4,0},{8,12},{12,8},{16,20},{20,16},{24,28},{28,24},{1,5},{5... | collective-permute-start | bytes 393224 | tf_op jit(solution)/shard_map/ppermute | solution.py:341
  102.9 2.2 %copy-done.1 = f32[2,128,4096]{2,1,0:T(8,128)S(1)} copy-done((f32[2,128,4096]{2,1,0:T(8,128)S(1)}, f32[2,128,4096]{2,1,0:T(8,128)}, u32[]{:S(2)}) %copy-start.1) | copy-done | bytes 4194328
  105.1 5.7 %apply.4.rest_0_ = f32[128,4096]{1,0:T(8,128)} custom-call(s32[1]{0:T(128)} %bitcast.me_ref, s32[1,3]{1,0:T(1,128)S(1)} %copy-done.6, s32[8,128]{1,0:T(8,128)S(1)} %bitcast.5, f32[128,384]{1,0:T(8,128)S(1)} %add.3.near_ref, f32[128,384]{1,0:T(8,128)S(1)} %collective-permute-done.10.far_ref, f32[2,128,4096]{2,1,0:T(8,128)S(1)} %copy-done.1, ...), custom_call_target="tpu_custom_call" | custom-call | flops 679477248 | bytes 4325376 | tf_op jit(solution)/shard_map/apply/pallas_call | solution.py:299
  110.8 0.0 collective-permute-done.18.yb_ref
  110.8 0.1 collective-permute-start.12
  110.9 0.0 collective-permute-done.19.za_ref
  110.9 4.4 %apply.5.rest_0_ = f32[128,4096]{1,0:T(8,128)} custom-call(s32[1]{0:T(128)} %bitcast.me_ref, s32[1,3]{1,0:T(1,128)S(1)} %copy-done.6, s32[8,128]{1,0:T(8,128)S(1)} %bitcast.6, f32[128,384]{1,0:T(8,128)S(1)} %add.3.near_ref, f32[128,384]{1,0:T(8,128)S(1)} %collective-permute-done.10.far_ref, ...), custom_call_target="tpu_custom_call", output_to_operand_aliasing={{}: (10, {})} | custom-call | flops 452984832 | bytes 2883584 | tf_op jit(solution)/shard_map/apply/pallas_call | solution.py:299
  115.3 0.0 collective-permute-done.16.za_ref
  115.3 4.4 %apply.6.rest_0_ = f32[128,4096]{1,0:T(8,128)} custom-call(s32[1]{0:T(128)} %bitcast.me_ref, s32[1,3]{1,0:T(1,128)S(1)} %copy-done.6, s32[8,128]{1,0:T(8,128)S(1)} %bitcast.7, f32[128,384]{1,0:T(8,128)S(1)} %add.3.near_ref, f32[128,384]{1,0:T(8,128)S(1)} %collective-permute-done.10.far_ref, ...), custom_call_target="tpu_custom_call", output_to_operand_aliasing={{}: (10, {})} | custom-call | flops 452984832 | bytes 2883584 | tf_op jit(solution)/shard_map/apply/pallas_call | solution.py:299
  119.8 0.0 collective-permute-done.12.yb_ref
  119.8 0.0 collective-permute-done.13.za_ref
  119.8 2.6 %apply.7 = f32[128,4096]{1,0:T(8,128)} custom-call(s32[1]{0:T(128)} %bitcast.me_ref, s32[1,3]{1,0:T(1,128)S(1)} %copy-done.6, s32[8,128]{1,0:T(8,128)S(1)} %bitcast.8, f32[128,384]{1,0:T(8,128)S(1)} %add.3.near_ref, f32[128,384]{1,0:T(8,128)S(1)} %collective-permute-done.10.far_ref, f32[2,128,4096]{2,1,0:T(8,128)S(1)} %copy-done.1, ...), custom_call_target="tpu_custom_call", output_to_operand_aliasing={{}: (10, {})} | custom-call | flops 226492416 | bytes 1441792 | tf_op jit(solution)/shard_map/apply/pallas_call | solution.py:299
  (20 shorter events, 0.0 us)
Async XLA Ops:
  3.0 17.4 %collective-permute-start.6 = (f32[128,1152]{1,0:T(8,128)}, f32[128,1152]{1,0:T(8,128)S(1)}, u32[]{:S(2)}, u32[]{:S(2)}) collective-permute-start(f32[128,1152]{1,0:T(8,128)} %get-tuple-element.29), channel_id=1, source_target_pairs={{0,4},{4,0},{8,12},{12,8},{16,20},{20,16},{24,28},{28,24},{1,5},{5... | collective-permute-start | bytes 1769480 | tf_op jit(solution)/shard_map/ppermute | solution.py:340
  9.0 24.0 %collective-permute-start = (f32[128,1152]{1,0:T(8,128)}, f32[128,1152]{1,0:T(8,128)S(1)}, u32[]{:S(2)}, u32[]{:S(2)}) collective-permute-start(f32[128,1152]{1,0:T(8,128)} %get-tuple-element.25), channel_id=1, source_target_pairs={{0,4},{4,0},{8,12},{12,8},{16,20},{20,16},{24,28},{28,24},{1,5},{5... | collective-permute-start | bytes 1769480 | tf_op jit(solution)/shard_map/ppermute | solution.py:340
  11.0 24.1 %copy-start.9 = (f32[128,256]{1,0:T(8,128)S(1)}, f32[128,256]{1,0:T(8,128)}, u32[]{:S(2)}) copy-start(f32[128,256]{1,0:T(8,128)} %get-tuple-element.28) | copy-start | bytes 393220
  11.0 45.1 %copy-start.7 = (f32[128,384]{1,0:T(8,128)S(1)}, f32[128,384]{1,0:T(8,128)}, u32[]{:S(2)}) copy-start(f32[128,384]{1,0:T(8,128)} %get-tuple-element.30) | copy-start | bytes 589828
  11.0 30.6 %collective-permute-start.3 = (f32[128,768]{1,0:T(8,128)}, f32[128,768]{1,0:T(8,128)}, u32[]{:S(2)}, u32[]{:S(2)}) collective-permute-start(f32[128,768]{1,0:T(8,128)} %get-tuple-element.27), channel_id=1, source_target_pairs={{0,4},{4,0},{8,12},{12,8},{16,20},{20,16},{24,28},{28,24},{1,5},{5... | collective-permute-start | bytes 1179656 | tf_op jit(solution)/shard_map/ppermute | solution.py:340
  16.1 47.5 %collective-permute-start.20 = (f32[128,1152]{1,0:T(8,128)}, f32[128,1152]{1,0:T(8,128)S(1)}, u32[]{:S(2)}, u32[]{:S(2)}) collective-permute-start(f32[128,1152]{1,0:T(8,128)} %get-tuple-element.42), channel_id=1, source_target_pairs={{0,4},{4,0},{8,12},{12,8},{16,20},{20,16},{24,28},{28,24},{1,5},{5... | collective-permute-start | bytes 1769480 | tf_op jit(solution)/shard_map/ppermute | solution.py:340
  20.4 43.9 %collective-permute-start.8 = (f32[128,1152]{1,0:T(8,128)S(1)}, f32[128,1152]{1,0:T(8,128)S(1)}, u32[]{:S(2)}, u32[]{:S(2)}) collective-permute-start(f32[128,1152]{1,0:T(8,128)S(1)} %collective-permute-done.6.ya_ref), channel_id=1, source_target_pairs={{0,8},{4,28},{8,16},{12,4},{16,24},{20,12},{24,0},{28,20},{1,9},{5... | collective-permute-start | bytes 1769480 | tf_op jit(solution)/shard_map/ppermute | solution.py:342
  33.0 26.7 %copy-start.3 = (f32[128,1152]{1,0:T(8,128)}, f32[128,1152]{1,0:T(8,128)S(1)}, u32[]{:S(2)}) copy-start(f32[128,1152]{1,0:T(8,128)S(1)} %collective-permute-done.ya_ref) | copy-start | bytes 1769476
  33.0 46.2 %collective-permute-start.2 = (f32[128,1152]{1,0:T(8,128)S(1)}, f32[128,1152]{1,0:T(8,128)}, u32[]{:S(2)}, u32[]{:S(2)}) collective-permute-start(f32[128,1152]{1,0:T(8,128)S(1)} %collective-permute-done.ya_ref), channel_id=1, source_target_pairs={{0,8},{4,28},{8,16},{12,4},{16,24},{20,12},{24,0},{28,20},{1,9},{5... | collective-permute-start | bytes 1769480 | tf_op jit(solution)/shard_map/ppermute | solution.py:342
  35.1 20.9 %collective-permute-start.4 = (f32[128,256]{1,0:T(8,128)S(1)}, f32[128,256]{1,0:T(8,128)S(1)}, u32[]{:S(2)}, u32[]{:S(2)}) collective-permute-start(f32[128,256]{1,0:T(8,128)S(1)} %copy-done.9), channel_id=1, source_target_pairs={{0,4},{4,0},{8,12},{12,8},{16,20},{20,16},{24,28},{28,24},{1,5},{5... | collective-permute-start | bytes 393224 | tf_op jit(solution)/shard_map/ppermute | solution.py:341
  41.6 31.7 %collective-permute-start.5 = (f32[128,768]{1,0:T(8,128)}, f32[128,768]{1,0:T(8,128)}, u32[]{:S(2)}, u32[]{:S(2)}) collective-permute-start(f32[128,768]{1,0:T(8,128)} %collective-permute-done.3.ya_ref), channel_id=1, source_target_pairs={{0,8},{4,28},{8,16},{12,4},{16,24},{20,12},{24,0},{28,20},{1,9},{5... | collective-permute-start | bytes 1179656 | tf_op jit(solution)/shard_map/ppermute | solution.py:342
  56.1 6.2 %collective-permute-start.7 = (f32[128,384]{1,0:T(8,128)S(1)}, f32[128,384]{1,0:T(8,128)S(1)}, u32[]{:S(2)}, u32[]{:S(2)}) collective-permute-start(f32[128,384]{1,0:T(8,128)S(1)} %copy-done.7), channel_id=1, source_target_pairs={{0,4},{4,0},{8,12},{12,8},{16,20},{20,16},{24,28},{28,24},{1,5},{5... | collective-permute-start | bytes 589832 | tf_op jit(solution)/shard_map/ppermute | solution.py:341
  59.8 5.9 %copy-start.2 = (f32[1,3,128,128]{3,2,1,0:T(8,128)S(1)}, f32[1,3,128,128]{3,2,1,0:T(8,128)}, u32[]{:S(2)}) copy-start(f32[1,3,128,128]{3,2,1,0:T(8,128)} %kernel_ref.5) | copy-start | bytes 589828
  59.8 5.9 %copy-start.5 = (s32[1024]{0:T(1024)S(1)}, s32[1024]{0:T(1024)}, u32[]{:S(2)}) copy-start(s32[1024]{0:T(1024)} %param.5) | copy-start | bytes 12292
  59.8 5.9 %copy-start.6 = (s32[1,3]{1,0:T(1,128)S(1)}, s32[1,3]{1,0:T(1,128)}, u32[]{:S(2)}) copy-start(s32[1,3]{1,0:T(1,128)} %pairs_ref.13) | copy-start | bytes 40
  62.2 17.0 %collective-permute-start.1 = (f32[128,384]{1,0:T(8,128)}, f32[128,384]{1,0:T(8,128)S(1)}, u32[]{:S(2)}, u32[]{:S(2)}) collective-permute-start(f32[128,384]{1,0:T(8,128)} %get-tuple-element.26), channel_id=1, source_target_pairs={{0,4},{4,0},{8,12},{12,8},{16,20},{20,16},{24,28},{28,24},{1,5},{5... | collective-permute-start | bytes 589832 | tf_op jit(solution)/shard_map/ppermute | solution.py:341
  63.6 24.6 %collective-permute-start.17 = (f32[128,768]{1,0:T(8,128)}, f32[128,768]{1,0:T(8,128)}, u32[]{:S(2)}, u32[]{:S(2)}) collective-permute-start(f32[128,768]{1,0:T(8,128)} %get-tuple-element.39), channel_id=1, source_target_pairs={{0,4},{4,0},{8,12},{12,8},{16,20},{20,16},{24,28},{28,24},{1,5},{5... | collective-permute-start | bytes 1179656 | tf_op jit(solution)/shard_map/ppermute | solution.py:340
  64.3 24.0 %collective-permute-start.14 = (f32[128,768]{1,0:T(8,128)}, f32[128,768]{1,0:T(8,128)}, u32[]{:S(2)}, u32[]{:S(2)}) collective-permute-start(f32[128,768]{1,0:T(8,128)} %get-tuple-element.37), channel_id=1, source_target_pairs={{0,4},{4,0},{8,12},{12,8},{16,20},{20,16},{24,28},{28,24},{1,5},{5... | collective-permute-start | bytes 1179656 | tf_op jit(solution)/shard_map/ppermute | solution.py:340
  65.7 2.2 %copy-start = (f32[2,128,4096]{2,1,0:T(8,128)S(1)}, f32[2,128,4096]{2,1,0:T(8,128)}, u32[]{:S(2)}) copy-start(f32[2,128,4096]{2,1,0:T(8,128)} %own_ref.13) | copy-start | bytes 12582916
  73.3 27.0 %collective-permute-start.22 = (f32[128,1152]{1,0:T(8,128)S(1)}, f32[128,1152]{1,0:T(8,128)}, u32[]{:S(2)}, u32[]{:S(2)}) collective-permute-start(f32[128,1152]{1,0:T(8,128)S(1)} %collective-permute-done.20.ya_ref), channel_id=1, source_target_pairs={{0,8},{4,28},{8,16},{12,4},{16,24},{20,12},{24,0},{28,20},{1,9},{5... | collective-permute-start | bytes 1769480 | tf_op jit(solution)/shard_map/ppermute | solution.py:342
  74.9 4.4 %copy-start.4 = (f32[128,1152]{1,0:T(8,128)S(1)}, f32[128,1152]{1,0:T(8,128)}, u32[]{:S(2)}) copy-start(f32[128,1152]{1,0:T(8,128)} %copy-done.3) | copy-start | bytes 1769476
  85.7 5.1 %collective-permute-start.9 = (f32[128,384]{1,0:T(8,128)}, f32[128,384]{1,0:T(8,128)S(1)}, u32[]{:S(2)}, u32[]{:S(2)}) collective-permute-start(f32[128,384]{1,0:T(8,128)} %get-tuple-element.33), channel_id=1, source_target_pairs={{0,1},{1,0},{2,3},{3,2},{4,5},{5,4},{6,7},{7,6},{8,9},{9,8},{10,11... | collective-permute-start | bytes 589832 | tf_op jit(solution)/shard_map/ppermute | solution.py:353
  85.7 15.2 %copy-start.8 = (f32[128,256]{1,0:T(8,128)S(1)}, f32[128,256]{1,0:T(8,128)}, u32[]{:S(2)}) copy-start(f32[128,256]{1,0:T(8,128)} %get-tuple-element.38) | copy-start | bytes 393220
  85.7 8.9 %collective-permute-start.21 = (f32[128,384]{1,0:T(8,128)}, f32[128,384]{1,0:T(8,128)}, u32[]{:S(2)}, u32[]{:S(2)}) collective-permute-start(f32[128,384]{1,0:T(8,128)} %get-tuple-element.43), channel_id=1, source_target_pairs={{0,4},{4,0},{8,12},{12,8},{16,20},{20,16},{24,28},{28,24},{1,5},{5... | collective-permute-start | bytes 589832 | tf_op jit(solution)/shard_map/ppermute | solution.py:341
  88.2 22.6 %collective-permute-start.19 = (f32[128,768]{1,0:T(8,128)}, f32[128,768]{1,0:T(8,128)}, u32[]{:S(2)}, u32[]{:S(2)}) collective-permute-start(f32[128,768]{1,0:T(8,128)} %collective-permute-done.17.ya_ref), channel_id=1, source_target_pairs={{0,8},{4,28},{8,16},{12,4},{16,24},{20,12},{24,0},{28,20},{1,9},{5... | collective-permute-start | bytes 1179656 | tf_op jit(solution)/shard_map/ppermute | solution.py:342
  88.3 27.1 %collective-permute-start.16 = (f32[128,768]{1,0:T(8,128)}, f32[128,768]{1,0:T(8,128)}, u32[]{:S(2)}, u32[]{:S(2)}) collective-permute-start(f32[128,768]{1,0:T(8,128)} %collective-permute-done.14.ya_ref), channel_id=1, source_target_pairs={{0,8},{4,28},{8,16},{12,4},{16,24},{20,12},{24,0},{28,20},{1,9},{5... | collective-permute-start | bytes 1179656 | tf_op jit(solution)/shard_map/ppermute | solution.py:342
  90.8 7.8 %collective-permute-start.11 = (f32[128,384]{1,0:T(8,128)}, f32[128,384]{1,0:T(8,128)S(1)}, u32[]{:S(2)}, u32[]{:S(2)}) collective-permute-start(f32[128,384]{1,0:T(8,128)} %get-tuple-element.34), channel_id=1, source_target_pairs={{0,4},{4,0},{8,12},{12,8},{16,20},{20,16},{24,28},{28,24},{1,5},{5... | collective-permute-start | bytes 589832 | tf_op jit(solution)/shard_map/ppermute | solution.py:340
  94.6 6.3 %collective-permute-start.10 = (f32[128,384]{1,0:T(8,128)S(1)}, f32[128,384]{1,0:T(8,128)S(1)}, u32[]{:S(2)}, u32[]{:S(2)}) collective-permute-start(f32[128,384]{1,0:T(8,128)S(1)} %add.3.near_ref), channel_id=1, source_target_pairs={{0,2},{1,3},{2,0},{3,1},{4,6},{5,7},{6,4},{7,5},{8,10},{9,11},{10,... | collective-permute-start | bytes 589832 | tf_op jit(solution)/shard_map/ppermute | solution.py:353
  98.6 12.2 %collective-permute-start.18 = (f32[128,256]{1,0:T(8,128)}, f32[128,256]{1,0:T(8,128)S(1)}, u32[]{:S(2)}, u32[]{:S(2)}) collective-permute-start(f32[128,256]{1,0:T(8,128)} %get-tuple-element.40), channel_id=1, source_target_pairs={{0,4},{4,0},{8,12},{12,8},{16,20},{20,16},{24,28},{28,24},{1,5},{5... | collective-permute-start | bytes 393224 | tf_op jit(solution)/shard_map/ppermute | solution.py:341
  100.4 19.4 %collective-permute-start.13 = (f32[128,384]{1,0:T(8,128)S(1)}, f32[128,384]{1,0:T(8,128)S(1)}, u32[]{:S(2)}, u32[]{:S(2)}) collective-permute-start(f32[128,384]{1,0:T(8,128)S(1)} %collective-permute-done.11.ya_ref), channel_id=1, source_target_pairs={{0,8},{4,28},{8,16},{12,4},{16,24},{20,12},{24,0},{28,20},{1,9},{5... | collective-permute-start | bytes 589832 | tf_op jit(solution)/shard_map/ppermute | solution.py:342
  100.9 14.4 %collective-permute-start.15 = (f32[128,256]{1,0:T(8,128)S(1)}, f32[128,256]{1,0:T(8,128)S(1)}, u32[]{:S(2)}, u32[]{:S(2)}) collective-permute-start(f32[128,256]{1,0:T(8,128)S(1)} %copy-done.8), channel_id=1, source_target_pairs={{0,4},{4,0},{8,12},{12,8},{16,20},{20,16},{24,28},{28,24},{1,5},{5... | collective-permute-start | bytes 393224 | tf_op jit(solution)/shard_map/ppermute | solution.py:341
  102.9 2.2 %copy-start.1 = (f32[2,128,4096]{2,1,0:T(8,128)S(1)}, f32[2,128,4096]{2,1,0:T(8,128)}, u32[]{:S(2)}) copy-start(f32[2,128,4096]{2,1,0:T(8,128)} %own_ref.13) | copy-start | bytes 12582916
  105.1 5.7 %copy-start.10 = (f32[128,128]{1,0:T(8,128)S(1)}, f32[128,128]{1,0:T(8,128)}, u32[]{:S(2)}) copy-start(f32[128,128]{1,0:T(8,128)} %get-tuple-element.35) | copy-start | bytes 196612
  110.8 9.0 %collective-permute-start.12 = (f32[128,128]{1,0:T(8,128)S(1)}, f32[128,128]{1,0:T(8,128)S(1)}, u32[]{:S(2)}, u32[]{:S(2)}) collective-permute-start(f32[128,128]{1,0:T(8,128)S(1)} %copy-done.10), channel_id=1, source_target_pairs={{0,4},{4,0},{8,12},{12,8},{16,20},{20,16},{24,28},{28,24},{1,5},{5... | collective-permute-start | bytes 196616 | tf_op jit(solution)/shard_map/ppermute | solution.py:341
